TPU v7x, 32 devices: a whole 2x2x4 slice. The times are simulated.
32 devices in a mesh: dp: 2 (over x), hist: 16 (over z, y, core).
Axes of the slice: x: 2, y: 2, z: 4, core: 2. Of those that a mesh axis runs over, the one named last changes fastest.
Arguments:
- queries: bfloat16 [2, 8192, 512], P('dp', 'hist'), may hold values from -6 to 6
- key_rows: bfloat16 [2, 8192, 512], P('dp', 'hist'), may hold values from -6 to 6
- value_rows: bfloat16 [2, 8192, 512], P('dp', 'hist'), may hold values from -6 to 6
- gate_rows: bfloat16 [2, 8192, 512], P('dp', 'hist'), may hold values from -6 to 6
- user_start: int32 [2, 8192], P('dp', 'hist'), may hold values from 0 to 8191, as said below
- w_out: bfloat16 [512, 1024], replicated, may hold values from -0.25 to 0.25
- out_grad: bfloat16 [2, 8192, 1024], P('dp', 'hist'), may hold values from -6 to 6
Outputs:
- query_grad: bfloat16 [2, 8192, 512], P('dp', 'hist')
- key_grad: bfloat16 [2, 8192, 512], P('dp', 'hist')
- value_grad: bfloat16 [2, 8192, 512], P('dp', 'hist')
- gate_grad: bfloat16 [2, 8192, 512], P('dp', 'hist')
- weight_grad: float32 [512, 1024], P('hist')
Inputs may be any that keep to these rules, and one draw needn't show every extreme that they name: user_start[g, i] is the position within group g of the first event of event i's user: it is at most i, never falls along the events, equals i where a user begins, and is 0 at the first event; the last event of every group is a user of its own.
All inputs are finite; a program needn't handle non-finite values.
Results may differ from a plain program's by a relative error of at most 0.012.
Values may be sent and summed in bfloat16 or wider, within the bound.
A program may use at most 128 MiB of HBM per device.

v0:
```python
import math

import jax
import jax.numpy as jnp
from jax import lax
from jax.sharding import PartitionSpec as P

HEADS = 4
HS = 128
WIN = 512


EPSILON = 1e-05


def shifted(value, axis, steps):
    count = lax.axis_size(axis)
    first, last = (max(0, -steps), min(count, count - steps))
    return lax.ppermute(value, axis, [(source, source + steps) for source in range(first, last)])


def split_heads(values):
    return values.reshape(values.shape[0], HEADS, HS)


def score_block(query_rows, key_piece):
    product = jnp.einsum(
        "rhd,chd->hrc",
        split_heads(query_rows),
        split_heads(key_piece),
        preferred_element_type=jnp.float32,
    )
    return product * HS ** (-0.5)


def window_mask(query_pos, start_rows, key_pos):
    spacing = query_pos[:, None] - key_pos[None, :]
    return (key_pos[None, :] >= start_rows[:, None]) & (spacing >= 0) & (spacing < WIN)


def silu_weights(scaled, live_map):
    sigmoid_s = jax.nn.sigmoid(scaled)
    weights = jnp.where(live_map[None], scaled * sigmoid_s / WIN, 0.0).astype(jnp.bfloat16)
    return (sigmoid_s, weights)


def attend(query_rows, key_piece, value_piece, live_map):
    scaled = score_block(query_rows, key_piece)
    sigmoid_s, weights = silu_weights(scaled, live_map)
    mixed = jnp.einsum(
        "hrc,chd->rhd", weights, split_heads(value_piece), preferred_element_type=jnp.float32
    )
    return mixed.reshape(query_rows.shape[0], -1)


def back_piece(query_rows, d_attn, key_piece, value_piece, live_map, want_keys):
    inv_root = HS ** (-0.5)
    scaled = score_block(query_rows, key_piece)
    sigmoid_s, weights = silu_weights(scaled, live_map)
    d_weights = jnp.einsum(
        "rhd,chd->hrc",
        split_heads(d_attn),
        split_heads(value_piece),
        preferred_element_type=jnp.float32,
    )
    d_scores = jnp.where(
        live_map[None], d_weights * sigmoid_s * (1.0 + scaled * (1.0 - sigmoid_s)) / WIN, 0.0
    )
    d_scores = d_scores.astype(jnp.bfloat16)
    results = []
    query_part = jnp.einsum(
        "hrc,chd->rhd", d_scores, split_heads(key_piece), preferred_element_type=jnp.float32
    )
    results.append(query_part.reshape(query_rows.shape[0], -1) * inv_root)
    key_part = jnp.einsum(
        "hrc,rhd->chd", d_scores, split_heads(query_rows), preferred_element_type=jnp.float32
    )
    value_part = jnp.einsum(
        "hrc,rhd->chd", weights, split_heads(d_attn), preferred_element_type=jnp.float32
    )
    results.append(key_part.reshape(want_keys, -1) * inv_root)
    results.append(value_part.reshape(want_keys, -1))
    return tuple(results)


def row_section(attended, gate_blk, grad_blk, w_out):
    row_mean = jnp.mean(attended, axis=-1, keepdims=True)
    centred = attended - row_mean
    inverse = lax.rsqrt(jnp.mean(centred * centred, axis=-1, keepdims=True) + EPSILON)
    normed = centred * inverse
    gate_wide = gate_blk.astype(jnp.float32)
    hidden = (normed * gate_wide).astype(jnp.bfloat16)
    d_hidden = lax.dot_general(
        grad_blk, w_out, (((1,), (1,)), ((), ())), preferred_element_type=jnp.float32
    )
    gate_grad = (d_hidden * normed).astype(jnp.bfloat16)
    d_normed = d_hidden * gate_wide
    d_attn = inverse * (
        d_normed
        - jnp.mean(d_normed, axis=-1, keepdims=True)
        - normed * jnp.mean(d_normed * normed, axis=-1, keepdims=True)
    )
    return (hidden, gate_grad, d_attn.astype(jnp.bfloat16))


def shards(queries, key_rows, value_rows, gate_rows, user_start, w_out, out_grad):
    query_loc = queries[0]
    key_loc = key_rows[0]
    value_loc = value_rows[0]
    gate_loc = gate_rows[0]
    start_loc = user_start[0]
    grad_loc = out_grad[0]
    ev_rows = query_loc.shape[0]
    tail = min(WIN, ev_rows)
    reach = -(-WIN // ev_rows)
    index = lax.axis_index("hist")
    hist_size = lax.axis_size("hist")
    row_ids = jnp.arange(ev_rows, dtype=jnp.int32)
    query_pos = index * ev_rows + row_ids
    tail_ids = jnp.arange(tail, dtype=jnp.int32) + (ev_rows - tail)
    offset = 1
    got_keys, got_values = shifted((key_loc, value_loc), "hist", offset)
    halo_pieces = [(got_keys, got_values, (index - offset) * ev_rows + tail_ids)]
    halo_live = [window_mask(query_pos, start_loc, member[2]) for member in halo_pieces]
    local_live = window_mask(query_pos, start_loc, query_pos)
    key_all = jnp.concatenate([member[0] for member in halo_pieces] + [key_loc], 0)
    value_all = jnp.concatenate([member[1] for member in halo_pieces] + [value_loc], 0)
    live_all = jnp.concatenate(halo_live + [local_live], 1)
    attended = attend(query_loc, key_all, value_all, live_all)
    hidden, gate_grad, d_attn = row_section(attended, gate_loc, grad_loc, w_out)
    want_all = reach * tail + ev_rows
    query_part, key_part, value_part = back_piece(
        query_loc, d_attn, key_all, value_all, live_all, want_all
    )
    local_key = key_part[want_all - ev_rows :]
    local_value = value_part[want_all - ev_rows :]
    remote_parts = [(key_part[0:tail], value_part[0:tail])]
    offset = 1
    got_key, got_value = shifted(
        (remote_parts[offset - 1][0], remote_parts[offset - 1][1]), "hist", -offset
    )
    key_total = local_key + got_key
    value_total = local_value + got_value
    weight_part = lax.psum_scatter(
        lax.dot_general(
            hidden, grad_loc, (((0,), (0,)), ((), ())), preferred_element_type=jnp.float32
        ),
        "hist",
        scatter_dimension=0,
        tiled=True,
    )
    weight_total = lax.psum(weight_part.astype(jnp.bfloat16), "dp").astype(jnp.float32)
    total_rows = lax.axis_size("dp") * hist_size * ev_rows
    weight_grad = weight_total / math.sqrt(total_rows)
    return (
        query_part.astype(jnp.bfloat16)[None],
        key_total.astype(jnp.bfloat16)[None],
        value_total.astype(jnp.bfloat16)[None],
        gate_grad[None],
        weight_grad,
    )


def solution(mesh):
    return jax.shard_map(
        shards,
        mesh=mesh,
        in_specs=(
            P("dp", "hist", None),
            P("dp", "hist", None),
            P("dp", "hist", None),
            P("dp", "hist", None),
            P("dp", "hist"),
            P(),
            P("dp", "hist", None),
        ),
        out_specs=(
            P("dp", "hist", None),
            P("dp", "hist", None),
            P("dp", "hist", None),
            P("dp", "hist", None),
            P("hist", None),
        ),
        check_vma=False,
    )
```

profile of v0, /device:TPU:1, one launch (start us, length us, event | category | flops | bytes accessed | tf_op | source)
XLA Modules:
  0.0 136.9 jit_solution(251763052997868147)
XLA Ops:
  7.2 0.0 copy-start
  7.2 0.0 reduce-scatter.2.cloned.1.call-start
  7.2 1.4 copy.31
  8.6 4.5 %collective-permute-start = (bf16[512,512]{0,1:T(8,128)(2,1)S(1)}, bf16[512,512]{0,1:T(8,128)(2,1)}, u32[]{:S(2)}, u32[]{:S(2)}) collective-permute-start(bf16[512,512]{0,1:T(8,128)(2,1)S(1)} %bitcast.106), channel_id=1, source_target_pairs={{0,1},{1,2},{2,3},{3,4},{4,5},{5,6},{6,7},{7,8},{8,9},{9,10},{10,1... | collective-permute-start | bytes 1572872 | tf_op jit(solution)/shard_map/ppermute | solution.py:19
  13.1 1.9 %collective-permute-start.1 = (bf16[512,512]{1,0:T(8,128)(2,1)}, bf16[512,512]{1,0:T(8,128)(2,1)}, u32[]{:S(2)}, u32[]{:S(2)}) collective-permute-start(bf16[512,512]{1,0:T(8,128)(2,1)} %bitcast.113), channel_id=1, source_target_pairs={{0,1},{1,2},{2,3},{3,4},{4,5},{5,6},{6,7},{7,8},{8,9},{9,10},{10,1... | collective-permute-start | bytes 1572872 | tf_op jit(solution)/shard_map/ppermute | solution.py:19
  15.1 2.1 %copy.36 = bf16[1,512,512]{1,2,0:T(8,128)(2,1)} copy(bf16[1,512,512]{2,1,0:T(8,128)(2,1)} %param.9) | data formatting | bytes 1048576 | tf_op args[2]
  17.1 1.0 copy.34
  18.1 1.3 copy.62
  19.4 0.2 copy.39
  19.6 0.7 fusion.18
  20.3 0.8 pad_add_fusion
  21.2 0.0 collective-permute-done
  21.2 1.3 copy.33
  22.5 0.0 copy-start.7
  22.5 7.5 %fusion.5 = (bf16[4,512,1024]{1,2,0:T(8,128)(2,1)}, f32[4,1024,512]{2,1,0:T(8,128)}) fusion(pred[512,1024]{0,1:T(8,128)(4,1)} %pad_add_fusion, bf16[512,4,128]{0,2,1:T(8,128)(2,1)S(1)} %bitcast.111, bf16[512,4,128]{2,0,1:T(8,128)(2,1)} %copy.34, bf16[512,4,128]{2,0,1:T(8,128)(2,1)S(1)} %copy.33), kind=kOutput, calls=%fused_computation.8 | convolution fusion | flops 555745280 | bytes 14680064 | tf_op jit(solution)/shard_map/rhd,chd->hrc/dot_general | solution.py:27
  30.0 0.0 collective-permute-done.1
  30.0 2.0 %copy.35 = bf16[512,512]{0,1:T(8,128)(2,1)} copy(bf16[512,512]{1,0:T(8,128)(2,1)} %collective-permute-done.1) | data formatting | bytes 1048576 | tf_op jit(solution)/shard_map/ppermute | solution.py:19
  32.1 3.1 %fusion.32 = (f32[512]{0:T(512)S(1)}, f32[4,128,512]{2,1,0:T(8,128)S(1)}) fusion(bf16[4,512,1024]{1,2,0:T(8,128)(2,1)} %get-tuple-element.25, bf16[512,4,128]{0,2,1:T(8,128)(2,1)S(1)} %bitcast.115, bf16[512,4,128]{0,2,1:T(8,128)(2,1)} %bitcast.116), kind=kOutput, calls=%fused_computation.62 | convolution fusion | flops 539229696 | bytes 6293504 | tf_op jit(solution)/shard_map/hrc,chd->rhd/dot_general | solution.py:50
  35.2 0.2 multiply_reduce_fusion.1
  35.3 0.2 multiply_convert_fusion
  35.5 2.0 %fusion.13 = f32[512,1024]{1,0:T(8,128)} fusion(bf16[512,512]{0,1:T(8,128)(2,1)S(1)} %bitcast.108, bf16[1,512,1024]{2,1,0:T(8,128)(2,1)S(1)} %copy-done), kind=kOutput, calls=%fused_computation.28 | convolution fusion | flops 536870912 | bytes 3670016 | tf_op jit(solution)/shard_map/dot_general | solution.py:145
  37.6 0.0 reduce-scatter.2.cloned.1.call-update
  37.6 0.0 all-reduce.2.cloned.1.call-start
  37.7 2.2 %fusion.25 = (f32[512]{0:T(512)S(1)}, f32[512]{0:T(512)S(1)}, f32[512,512]{0,1:T(8,128)S(1)}) fusion(bf16[1,512,512]{1,2,0:T(8,128)(2,1)S(1)} %copy.39, f32[512]{0:T(512)S(1)} %add_rsqrt_fusion, f32[512]{0:T(512)S(1)} %broadcast_multiply_fusion.2, f32[4,128,512]{2,1,0:T(8,128)S(1)} %get-tuple-element.28, bf16[512,1024]{1,0:T(8,128)(2,1)} %param.12, ...), kind=kOutput, calls=%fused_computation.48 | convolution fusion | flops 538704896 | bytes 4726784 | tf_op jit(solution)/shard_map/dot_general | solution.py:93
  39.9 1.2 multiply_convert_fusion.1
  41.1 1.5 %convolution_bitcast_fusion = f32[1024,4,128]{0,2,1:T(8,128)S(1)} fusion(bf16[512,4,128]{0,2,1:T(8,128)(2,1)S(1)} %bitcast.109, bf16[4,512,1024]{1,2,0:T(8,128)(2,1)S(1)} %copy-done.1), kind=kOutput, calls=%fused_computation.16 | convolution fusion | flops 536870912 | bytes 6815744 | tf_op jit(solution)/shard_map/hrc,rhd->chd/dot_general | solution.py:78
  42.6 0.2 fusion.30
  42.8 1.4 %copy.50 = f32[512,512]{1,0:T(8,128)} copy(f32[512,512]{0,1:T(8,128)S(1)} %bitcast.103) | data formatting | bytes 2097152 | tf_op jit(solution)/shard_map/slice | solution.py:137
  44.2 3.4 %collective-permute-start.3 = (f32[512,512]{1,0:T(8,128)}, f32[512,512]{1,0:T(8,128)}, u32[]{:S(2)}, u32[]{:S(2)}) collective-permute-start(f32[512,512]{1,0:T(8,128)} %copy.50), channel_id=1, source_target_pairs={{1,0},{2,1},{3,2},{4,3},{5,4},{6,5},{7,6},{8,7},{9,8},{10,9},{11,1... | collective-permute-start | bytes 3145736 | tf_op jit(solution)/shard_map/ppermute | solution.py:19
  47.6 7.5 %fusion.10 = bf16[4,512,1024]{1,2,0:T(8,128)(2,1)S(1)} fusion(f32[4,1024,512]{2,1,0:T(8,128)} %get-tuple-element.26, pred[512,1024]{0,1:T(8,128)(4,1)} %pad_add_fusion, bf16[512,4,128]{0,2,1:T(8,128)(2,1)} %bitcast.110, bf16[512,4,128]{0,2,1:T(8,128)(2,1)} %bitcast.114, bf16[512,4,128]{0,2,1:T(8,128)(2,1)} %bitcast.117), kind=kOutput, calls=%fused_computation.13 | convolution fusion | flops 564133888 | bytes 14680064 | tf_op jit(solution)/shard_map/rhd,chd->hrc/dot_general | solution.py:60
  55.1 1.5 %multiply_bitcast_fusion = f32[1024,4,128]{0,2,1:T(8,128)S(1)} fusion(bf16[4,512,1024]{1,2,0:T(8,128)(2,1)S(1)} %fusion.10, bf16[512,4,128]{0,2,1:T(8,128)(2,1)S(1)} %bitcast.112), kind=kOutput, calls=%fused_computation.14 | convolution fusion | flops 537395200 | bytes 6815744 | tf_op jit(solution)/shard_map/hrc,rhd->chd/dot_general | solution.py:75
  56.6 1.1 fusion.31
  57.8 1.3 copy.47
  59.1 1.9 %collective-permute-start.2 = (f32[512,512]{1,0:T(8,128)}, f32[512,512]{1,0:T(8,128)}, u32[]{:S(2)}, u32[]{:S(2)}) collective-permute-start(f32[512,512]{1,0:T(8,128)} %copy.47), channel_id=1, source_target_pairs={{1,0},{2,1},{3,2},{4,3},{5,4},{6,5},{7,6},{8,7},{9,8},{10,9},{11,1... | collective-permute-start | bytes 3145736 | tf_op jit(solution)/shard_map/ppermute | solution.py:19
  61.0 0.3 copy.51
  61.3 1.6 %copy.48 = f32[512,512]{1,0:T(8,128)S(1)} copy(f32[512,512]{0,1:T(8,128)} %bitcast.102) | data formatting | bytes 2097152 | tf_op jit(solution)/shard_map/slice | solution.py:135
  62.9 4.1 %fusion.11 = bf16[4,128,512]{2,1,0:T(8,128)(2,1)} fusion(bf16[4,512,1024]{1,2,0:T(8,128)(2,1)} %copy-done.2, bf16[512,4,128]{2,0,1:T(8,128)(2,1)} %copy.34, bf16[512,4,128]{2,0,1:T(8,128)(2,1)} %copy-done.8), kind=kOutput, calls=%fused_computation.22 | convolution fusion | flops 539492352 | bytes 5767168 | tf_op jit(solution)/shard_map/hrc,chd->rhd/dot_general | solution.py:71
  67.0 2.0 %copy.52 = bf16[1,512,512]{2,1,0:T(8,128)(2,1)} copy(bf16[1,512,512]{1,2,0:T(8,128)(2,1)} %bitcast.118) | data formatting | bytes 1048576
  69.1 2.0 %copy.53 = bf16[1,512,512]{2,1,0:T(8,128)(2,1)} copy(bf16[1,512,512]{1,2,0:T(8,128)(2,1)} %bitcast.105) | data formatting | bytes 1048576
  71.1 0.0 collective-permute-done.3
  71.1 2.2 %fusion.24 = bf16[1,512,512]{2,1,0:T(8,128)(2,1)} fusion(f32[512,512]{1,0:T(8,128)S(1)} %copy.51, f32[512,512]{1,0:T(8,128)} %collective-permute-done.3), kind=kLoop, calls=%fused_computation.47 | loop fusion | flops 524288 | bytes 2621440 | tf_op jit(solution)/shard_map/broadcast_in_dim | solution.py:158
  73.3 31.1 %reduce-scatter.2.cloned.1.call-done = f32[32,1024]{1,0:T(8,128)} async-done(((f32[512,1024]{1,0:T(8,128)}), f32[32,1024]{1,0:T(8,128)}) %reduce-scatter.2.cloned.1.call-update) | async-done | bytes 131088 | tf_op jit(solution)/shard_map/reduce_scatter | solution.py:144
  104.4 1.5 %convert_element_type.74 = bf16[32,1024]{1,0:T(8,128)(2,1)} convert(f32[32,1024]{1,0:T(8,128)} %reduce-scatter.2.cloned.1.call-done) | non-fusion elementwise | flops 32768 | bytes 196608 | tf_op jit(solution)/shard_map/convert_element_type | solution.py:152
  106.0 0.0 all-reduce.2.cloned.1.call-update
  106.0 0.0 collective-permute-done.2
  106.0 2.2 %fusion.23 = bf16[1,512,512]{2,1,0:T(8,128)(2,1)} fusion(f32[512,512]{1,0:T(8,128)S(1)} %copy.48, f32[512,512]{1,0:T(8,128)} %collective-permute-done.2), kind=kLoop, calls=%fused_computation.46 | loop fusion | flops 524288 | bytes 2621440 | tf_op jit(solution)/shard_map/broadcast_in_dim | solution.py:157
  108.2 20.4 %all-reduce.2.cloned.1.call-done = bf16[32,1024]{1,0:T(8,128)(2,1)} async-done(((bf16[32,1024]{1,0:T(8,128)(2,1)}), bf16[32,1024]{1,0:T(8,128)(2,1)}) %all-reduce.2.cloned.1.call-update) | async-done | bytes 65552 | tf_op jit(solution)/shard_map/psum | solution.py:152
  128.5 1.5 %convert_multiply_fusion = f32[32,1024]{1,0:T(8,128)} fusion(bf16[32,1024]{1,0:T(8,128)(2,1)} %all-reduce.2.cloned.1.call-done), kind=kLoop, calls=%fused_computation.49 | loop fusion | flops 65536 | bytes 196608 | tf_op jit(solution)/shard_map/div | solution.py:154
  (23 shorter events, 0.1 us)
Async XLA Ops:
  7.2 28.4 %copy-start = (bf16[1,512,1024]{2,1,0:T(8,128)(2,1)S(1)}, bf16[1,512,1024]{2,1,0:T(8,128)(2,1)}, u32[]{:S(2)}) copy-start(bf16[1,512,1024]{2,1,0:T(8,128)(2,1)} %param.13) | copy-start | bytes 3145732
  7.2 12.2 %copy-start.6 = (bf16[1,512,512]{2,1,0:T(8,128)(2,1)S(1)}, bf16[1,512,512]{2,1,0:T(8,128)(2,1)}, u32[]{:S(2)}) copy-start(bf16[1,512,512]{2,1,0:T(8,128)(2,1)} %param.10) | copy-start | bytes 1572868
  7.2 12.5 %copy-start.9 = (s32[1,512]{1,0:T(1,128)S(1)}, s32[1,512]{1,0:T(1,128)}, u32[]{:S(2)}) copy-start(s32[1,512]{1,0:T(1,128)} %param.11) | copy-start | bytes 6148
  7.2 97.2 %reduce-scatter.2.cloned.1.call-start = ((), (), s32[]{:S(2)}) async-start(), calls=%async_computation.1 | async-start | bytes 2228224 | tf_op jit(solution)/shard_map/reduce_scatter | solution.py:144
  8.6 12.6 %collective-permute-start = (bf16[512,512]{0,1:T(8,128)(2,1)S(1)}, bf16[512,512]{0,1:T(8,128)(2,1)}, u32[]{:S(2)}, u32[]{:S(2)}) collective-permute-start(bf16[512,512]{0,1:T(8,128)(2,1)S(1)} %bitcast.106), channel_id=1, source_target_pairs={{0,1},{1,2},{2,3},{3,4},{4,5},{5,6},{6,7},{7,8},{8,9},{9,10},{10,1... | collective-permute-start | bytes 1572872 | tf_op jit(solution)/shard_map/ppermute | solution.py:19
  13.1 16.9 %collective-permute-start.1 = (bf16[512,512]{1,0:T(8,128)(2,1)}, bf16[512,512]{1,0:T(8,128)(2,1)}, u32[]{:S(2)}, u32[]{:S(2)}) collective-permute-start(bf16[512,512]{1,0:T(8,128)(2,1)} %bitcast.113), channel_id=1, source_target_pairs={{0,1},{1,2},{2,3},{3,4},{4,5},{5,6},{6,7},{7,8},{8,9},{9,10},{10,1... | collective-permute-start | bytes 1572872 | tf_op jit(solution)/shard_map/ppermute | solution.py:19
  19.4 10.6 %copy-start.4 = (bf16[1,512,512]{1,2,0:T(8,128)(2,1)}, bf16[1,512,512]{1,2,0:T(8,128)(2,1)S(1)}, u32[]{:S(2)}) copy-start(bf16[1,512,512]{1,2,0:T(8,128)(2,1)S(1)} %copy.62) | copy-start | bytes 1572868
  22.5 7.5 %copy-start.8 = (bf16[512,4,128]{2,0,1:T(8,128)(2,1)}, bf16[512,4,128]{2,0,1:T(8,128)(2,1)S(1)}, u32[]{:S(2)}) copy-start(bf16[512,4,128]{2,0,1:T(8,128)(2,1)S(1)} %copy.33) | copy-start | bytes 1572868
  22.5 9.6 %copy-start.7 = (bf16[1,512,512]{1,2,0:T(8,128)(2,1)S(1)}, bf16[1,512,512]{1,2,0:T(8,128)(2,1)}, u32[]{:S(2)}) copy-start(bf16[1,512,512]{1,2,0:T(8,128)(2,1)} %copy.36) | copy-start | bytes 1572868
  37.6 90.9 %all-reduce.2.cloned.1.call-start = ((), (), s32[]{:S(2)}) async-start(), calls=%async_computation.2 | async-start | bytes 131072 | tf_op jit(solution)/shard_map/psum | solution.py:152
  37.7 3.4 %copy-start.1 = (bf16[4,512,1024]{1,2,0:T(8,128)(2,1)S(1)}, bf16[4,512,1024]{1,2,0:T(8,128)(2,1)}, u32[]{:S(2)}) copy-start(bf16[4,512,1024]{1,2,0:T(8,128)(2,1)} %get-tuple-element.25) | copy-start | bytes 12582916
  41.1 1.7 %copy-start.3 = (bf16[512,512]{0,1:T(8,128)(2,1)}, bf16[512,512]{0,1:T(8,128)(2,1)S(1)}, u32[]{:S(2)}) copy-start(bf16[512,512]{0,1:T(8,128)(2,1)S(1)} %get-tuple-element.18) | copy-start | bytes 1572868
  44.2 26.9 %collective-permute-start.3 = (f32[512,512]{1,0:T(8,128)}, f32[512,512]{1,0:T(8,128)}, u32[]{:S(2)}, u32[]{:S(2)}) collective-permute-start(f32[512,512]{1,0:T(8,128)} %copy.50), channel_id=1, source_target_pairs={{1,0},{2,1},{3,2},{4,3},{5,4},{6,5},{7,6},{8,7},{9,8},{10,9},{11,1... | collective-permute-start | bytes 3145736 | tf_op jit(solution)/shard_map/ppermute | solution.py:19
  47.6 7.6 %copy-start.5 = (bf16[1,512,512]{1,2,0:T(8,128)(2,1)S(1)}, bf16[1,512,512]{1,2,0:T(8,128)(2,1)}, u32[]{:S(2)}) copy-start(bf16[1,512,512]{1,2,0:T(8,128)(2,1)} %copy-done.4) | copy-start | bytes 1572868
  55.1 2.6 %copy-start.2 = (bf16[4,512,1024]{1,2,0:T(8,128)(2,1)}, bf16[4,512,1024]{1,2,0:T(8,128)(2,1)S(1)}, u32[]{:S(2)}) copy-start(bf16[4,512,1024]{1,2,0:T(8,128)(2,1)S(1)} %fusion.10) | copy-start | bytes 12582916
  59.1 46.9 %collective-permute-start.2 = (f32[512,512]{1,0:T(8,128)}, f32[512,512]{1,0:T(8,128)}, u32[]{:S(2)}, u32[]{:S(2)}) collective-permute-start(f32[512,512]{1,0:T(8,128)} %copy.47), channel_id=1, source_target_pairs={{1,0},{2,1},{3,2},{4,3},{5,4},{6,5},{7,6},{8,7},{9,8},{10,9},{11,1... | collective-permute-start | bytes 3145736 | tf_op jit(solution)/shard_map/ppermute | solution.py:19
Sparse Core Ops, SparseCore 0:
  37.7 66.6 reduce-scatter.1
  107.2 21.2 all-reduce.1
where the time goes:
time: 139 us; the launch traced here: 137 us
  waiting for transfers between devices  51.5 us (37%)
  matrix products  29.4 us (21%)
  local copies, waits for them, and re-layouts  19.3 us (14%)
  between operations  14.3 us (10%)
  starting transfers between devices  11.8 us (8%)
  other arithmetic  10.5 us (8%)
    reduce_scatter x1, waiting for transfers between devices, shards(): lax.psum_scatter(lax.dot_general(hidden, grad_loc, (((0,), (0,)), ((), ()...  31.1 us
    psum x1, waiting for transfers between devices, shards(): lax.psum(weight_part.astype(jnp.bfloat16), 'dp').astype(jnp.float32)  20.4 us
    ppermute x4, starting transfers between devices, shifted(): lax.ppermute(value, axis, [(source, source + steps) for source in range(f...  11.7 us
    unnamed x25, local copies, waits for them, and re-layouts  7.77 us
    dot_general x1, matrix products, back_piece(): jnp.einsum('rhd,chd->hrc', split_heads(d_attn), split_heads(value_piece),...  7.54 us
    dot_general x1, matrix products, score_block(): jnp.einsum('rhd,chd->hrc', split_heads(query_rows), split_heads(key_piece...  7.48 us
    dot_general x1, matrix products, back_piece(): jnp.einsum('hrc,chd->rhd', d_scores, split_heads(key_piece), preferred_el...  4.13 us
    slice x4, local copies, waits for them, and re-layouts, shards(): remote_parts = [(key_part[0:tail], value_part[0:tail])]  4.07 us
  transfers between devices with their start and end apart: 6, of which 2 were waited for; matrix products, arithmetic and copies ran while one was open for 36% of the time, Pallas kernels for 0%

commit v1 on v0

v1 whole, which is shorter than its diff:
```python
import functools
import math

import jax
import jax.numpy as jnp
from jax import lax
from jax.experimental import pallas as pl
from jax.experimental.pallas import tpu as pltpu
from jax.sharding import PartitionSpec as P

HEADS = 4
HS = 128
WIN = 512
EPSILON = 1e-05
BF = jnp.bfloat16
F32 = jnp.float32


def dot(a, b, ca, cb):
    return lax.dot_general(a, b, (((ca,), (cb,)), ((), ())), preferred_element_type=F32)


def kernel(
    n, dp, total_rows,
    q_ref, k_ref, v_ref, u_ref, st_ref, w_ref, go_ref,
    dq_ref, dk_ref, dv_ref, du_ref, dw_ref,
    halo, w_s, g_s, att, dh, da, hid, out_kv, in_kv, wp, *rest,
):
    steps = n.bit_length() - 1
    dsteps = dp.bit_length() - 1
    hops = steps + dsteps
    sends, recvs = rest[:hops], rest[hops : 2 * hops]
    ks, kr, gs, gr, ws, wr = rest[2 * hops :]
    ev = q_ref.shape[0]
    blk = ev // 2
    me = lax.axis_index("hist")
    mine = lax.axis_index("dp")
    has_left = me > 0
    has_right = me < n - 1
    mesh = pl.DeviceIdType.MESH

    def xor(value, bit):
        return value + bit - 2 * bit * ((value // bit) % 2)

    partners = [{"hist": xor(me, 1 << s)} for s in range(steps)]
    partners += [{"dp": xor(mine, 1 << s)} for s in range(dsteps)]

    barrier = pltpu.get_barrier_semaphore()
    for partner in partners:
        pl.semaphore_signal(barrier, inc=1, device_id=partner, device_id_type=mesh)

    @pl.when(has_right)
    def _():
        pl.semaphore_signal(barrier, inc=1, device_id={"hist": me + 1}, device_id_type=mesh)

    @pl.when(has_left)
    def _():
        pl.semaphore_signal(barrier, inc=1, device_id={"hist": me - 1}, device_id_type=mesh)

    pl.semaphore_wait(barrier, hops + has_left.astype(jnp.int32) + has_right.astype(jnp.int32))

    halo_copies = [
        pltpu.make_async_remote_copy(
            src_ref=ref, dst_ref=halo.at[i], send_sem=ks.at[i], recv_sem=kr.at[i],
            device_id={"hist": me + 1}, device_id_type=mesh,
        )
        for i, ref in enumerate((k_ref, v_ref))
    ]
    grad_copies = [
        pltpu.make_async_remote_copy(
            src_ref=out_kv.at[h], dst_ref=in_kv.at[h], send_sem=gs.at[h], recv_sem=gr.at[h],
            device_id={"hist": me - 1}, device_id_type=mesh,
        )
        for h in range(HEADS)
    ]
    sum_copies = [
        pltpu.make_async_remote_copy(
            src_ref=sends[s], dst_ref=recvs[s], send_sem=ws.at[s], recv_sem=wr.at[s],
            device_id=partners[s], device_id_type=mesh,
        )
        for s in range(hops)
    ]

    @pl.when(has_right)
    def _():
        for copy in halo_copies:
            copy.start()

    @pl.when(me == 0)
    def _():
        halo[...] = jnp.zeros_like(halo)

    @pl.when(me == n - 1)
    def _():
        in_kv[...] = jnp.zeros_like(in_kv)

    scale = HS ** (-0.5)
    base = me * ev

    def head(h):
        return slice(h * HS, (h + 1) * HS)

    def mask(part, b, lo, hi):
        cols = slice(b * blk, (b + 1) * blk)
        start = st_ref[:, cols] - base
        jj = lax.broadcasted_iota(jnp.int32, (hi - lo, blk), 0) + lo
        ii = lax.broadcasted_iota(jnp.int32, (hi - lo, blk), 1) + b * blk
        if part == 0:
            live = (jj >= start + ev) & (jj > ii)
        else:
            live = (jj >= start) & (jj <= ii)
        return jnp.where(live, 1.0 / WIN, 0.0).astype(F32)

    def span(part, b):
        return (b * blk, ev) if part == 0 else (0, (b + 1) * blk)

    def scores(part, b, h, keys, live):
        lo, hi = span(part, b)
        cols = slice(b * blk, (b + 1) * blk)
        x = dot(keys[lo:hi, head(h)], q_ref[cols, head(h)], 1, 1) * scale
        sig = 0.5 * jnp.tanh(0.5 * x) + 0.5
        part_sig = sig * live
        wt = x * part_sig
        g_s[h, part, lo:hi, cols] = (part_sig + wt * (1.0 - sig)).astype(BF)
        w_s[h, part, lo:hi, cols] = wt.astype(BF)

    def mix(part, b, h, values):
        lo, hi = span(part, b)
        cols = slice(b * blk, (b + 1) * blk)
        return dot(w_s[h, part, lo:hi, cols], values[lo:hi, head(h)], 0, 0)

    for b in range(2):
        live = mask(1, b, *span(1, b))
        for h in range(HEADS):
            scores(1, b, h, k_ref, live)
            att[b * blk : (b + 1) * blk, head(h)] = mix(1, b, h, v_ref)
    for b in range(2):
        rows = slice(b * blk, (b + 1) * blk)
        dh[rows, :] = dot(go_ref[rows, :], w_ref[...], 1, 1)

    @pl.when(has_left)
    def _():
        halo_copies[0].wait_recv()

    for b in range(2):
        live = mask(0, b, *span(0, b))
        for h in range(HEADS):
            scores(0, b, h, halo.at[0], live)

    @pl.when(has_left)
    def _():
        halo_copies[1].wait_recv()

    for b in range(2):
        for h in range(HEADS):
            att[b * blk : (b + 1) * blk, head(h)] += mix(0, b, h, halo.at[1])

    chunk = 64
    @pl.loop(0, ev // chunk)
    def _(c):
        rows = pl.ds(pl.multiple_of(c * chunk, chunk), chunk)
        a = att[rows, :]
        centred = a - jnp.mean(a, axis=-1, keepdims=True)
        inverse = lax.rsqrt(jnp.mean(centred * centred, axis=-1, keepdims=True) + EPSILON)
        normed = centred * inverse
        gate = u_ref[rows, :].astype(F32)
        hid[rows, :] = (normed * gate).astype(BF)
        d_hidden = dh[rows, :]
        du_ref[rows, :] = (d_hidden * normed).astype(BF)
        d_normed = d_hidden * gate
        d_attn = inverse * (
            d_normed
            - jnp.mean(d_normed, axis=-1, keepdims=True)
            - normed * jnp.mean(d_normed * normed, axis=-1, keepdims=True)
        )
        da[rows, :] = d_attn.astype(BF)

    block_rows = wp.shape[1]

    def weight_part():
        cols = hid.shape[1] // 2
        for b in range(2):
            piece = dot(hid[:, b * cols : (b + 1) * cols], go_ref[...], 0, 0)
            wp[b * n // 2 : (b + 1) * n // 2] = piece.reshape(n // 2, block_rows, piece.shape[1])

    def launch(s):
        if s < steps:
            count = n >> (s + 1)
            bit = (me // (1 << s)) % 2
            for i in range(count):
                sends[s][i] = wp[2 * i + 1 - bit].astype(BF)
        else:
            sends[s][0] = wp[0].astype(BF)
        sum_copies[s].start()

    def land(s):
        sum_copies[s].wait_recv()
        if s < steps:
            count = n >> (s + 1)
            bit = (me // (1 << s)) % 2
            for i in range(count):
                wp[i] = wp[2 * i + bit] + recvs[s][i].astype(F32)
        else:
            wp[0] = sends[s][0].astype(F32) + recvs[s][0].astype(F32)

    def queries(part, kb):
        return slice(0, (kb + 1) * blk) if part == 0 else slice(kb * blk, ev)

    def back(part, h, keep):
        values = halo.at[1] if part == 0 else v_ref
        for kb in range(2):
            rows = slice(kb * blk, (kb + 1) * blk)
            cols = queries(part, kb)
            d_rows = da[cols, head(h)]
            d_w = dot(values[rows, head(h)], d_rows, 1, 1)
            d_s = (d_w * g_s[h, part, rows, cols].astype(F32)).astype(BF)
            g_s[h, part, rows, cols] = d_s
            d_k = dot(d_s, q_ref[cols, head(h)], 1, 0) * scale
            d_v = dot(w_s[h, part, rows, cols], d_rows, 1, 0)
            keep(h, rows, d_k, d_v)

    def keep_far(h, rows, d_k, d_v):
        out_kv[h, 0, rows, :] = d_k.astype(BF)
        out_kv[h, 1, rows, :] = d_v.astype(BF)

    def far(h):
        back(0, h, keep_far)

        @pl.when(has_left)
        def _():
            grad_copies[h].start()

    def keep_near(h, rows, d_k, d_v):
        att[rows, head(h)] = d_k
        dh[rows, head(h)] = d_v

    def near(h):
        back(1, h, keep_near)

    def query_side(h):
        for b in range(2):
            cols = slice(b * blk, (b + 1) * blk)
            total = 0.0
            for part, keys in ((0, halo.at[0]), (1, k_ref)):
                lo, hi = span(part, b)
                total = total + dot(g_s[h, part, lo:hi, cols], keys[lo:hi, head(h)], 0, 0)
            dq_ref[cols, head(h)] = (total * scale).astype(BF)

    def finish(h):
        @pl.when(has_right)
        def _():
            grad_copies[h].wait_recv()

        dk_ref[:, head(h)] = (att[:, head(h)] + in_kv[h, 0].astype(F32)).astype(BF)
        dv_ref[:, head(h)] = (dh[:, head(h)] + in_kv[h, 1].astype(F32)).astype(BF)

    weight_part()
    launch(0)
    work = [(far, 0), (far, 1), (far, 2), (far, 3)]
    work += [(near, 0), (near, 1), (near, 2), (near, 3)]
    work += [(query_side, 0), (query_side, 1), (query_side, 2), (query_side, 3)]
    pending = 0
    for i, (task, h) in enumerate(work):
        task(h)
        if i % 3 == 2 or i == 1:
            if pending < hops - 1:
                land(pending)
                pending += 1
                launch(pending)
    while pending < hops - 1:
        land(pending)
        pending += 1
        launch(pending)
    for h in range(HEADS):
        finish(h)
    land(hops - 1)
    dw_ref[...] = wp[0] / math.sqrt(total_rows)

    @pl.when(has_right)
    def _():
        for copy in halo_copies:
            copy.wait_send()

    @pl.when(has_left)
    def _():
        for copy in grad_copies:
            copy.wait_send()

    for copy in sum_copies:
        copy.wait_send()


def shards(n, dp, queries, key_rows, value_rows, gate_rows, user_start, w_out, out_grad):
    ev, width = queries.shape[1:]
    model = w_out.shape[1]
    block_rows = width // n
    steps = n.bit_length() - 1
    dsteps = dp.bit_length() - 1
    hops = steps + dsteps
    sizes = [n >> (s + 1) for s in range(steps)] + [1] * dsteps
    legs = [pltpu.VMEM((size, block_rows, model), BF) for size in sizes]
    rows = jax.ShapeDtypeStruct((ev, width), BF)
    vmem = pl.BlockSpec(memory_space=pltpu.VMEM)
    dma = pltpu.SemaphoreType.DMA
    results = pl.pallas_call(
        functools.partial(kernel, n, dp, dp * n * ev),
        out_shape=(rows, rows, rows, rows, jax.ShapeDtypeStruct((block_rows, model), F32)),
        in_specs=[vmem] * 7,
        out_specs=(vmem,) * 5,
        scratch_shapes=[
            pltpu.VMEM((2, ev, width), BF),
            pltpu.VMEM((HEADS, 2, ev, ev), BF),
            pltpu.VMEM((HEADS, 2, ev, ev), BF),
            pltpu.VMEM((ev, width), F32),
            pltpu.VMEM((ev, width), F32),
            pltpu.VMEM((ev, width), BF),
            pltpu.VMEM((ev, width), BF),
            pltpu.VMEM((HEADS, 2, ev, HS), BF),
            pltpu.VMEM((HEADS, 2, ev, HS), BF),
            pltpu.VMEM((n, block_rows, model), F32),
        ]
        + legs
        + legs
        + [dma((2,)), dma((2,)), dma((HEADS,)), dma((HEADS,)), dma((hops,)), dma((hops,))],
        compiler_params=pltpu.CompilerParams(
            collective_id=0, has_side_effects=True, vmem_limit_bytes=60 * 1024 * 1024
        ),
    )(
        queries[0], key_rows[0], value_rows[0], gate_rows[0], user_start, w_out, out_grad[0]
    )
    return tuple(r[None] for r in results[:4]) + (results[4],)


def solution(mesh):
    n, dp = mesh.shape["hist"], mesh.shape["dp"]
    return jax.shard_map(
        functools.partial(shards, n, dp),
        mesh=mesh,
        in_specs=(
            P("dp", "hist", None),
            P("dp", "hist", None),
            P("dp", "hist", None),
            P("dp", "hist", None),
            P("dp", "hist"),
            P(),
            P("dp", "hist", None),
        ),
        out_specs=(
            P("dp", "hist", None),
            P("dp", "hist", None),
            P("dp", "hist", None),
            P("dp", "hist", None),
            P("hist", None),
        ),
        check_vma=False,
    )
```

time: 139 us -> 63.4 us (0.46)
  the two profiles are of different devices: /device:TPU:1 before, /device:TPU:20 now
where the time goes in v1:
time: 63.4 us; the launch traced here: 63.1 us
  Pallas kernels  56.4 us (89%)
  local copies, waits for them, and re-layouts  6.07 us (10%)
  between operations  0.66 us (1%)
    pallas_call x1, Pallas kernels, shards(): pl.pallas_call(functools.partial(kernel, n, dp, dp * n * ev), out_shape=(...  56.4 us
    unnamed x13, local copies, waits for them, and re-layouts  6.07 us

profile of v1, /device:TPU:20, one launch (start us, length us, event | category | flops | bytes accessed | tf_op | source)
XLA Modules:
  0.0 63.1 jit_solution(9582604391334185977)
XLA Ops:
  0.6 56.4 %shard_map.110 = (bf16[512,512]{1,0:T(8,128)(2,1)}, bf16[512,512]{1,0:T(8,128)(2,1)}, bf16[512,512]{1,0:T(8,128)(2,1)}, bf16[512,512]{1,0:T(8,128)(2,1)}, f32[32,1024]{1,0:T(8,128)}) custom-call(bf16[512,512]{1,0:T(8,128)(2,1)} %bitcast.14, bf16[512,512]{1,0:T(8,128)(2,1)} %bitcast.15, bf16[512,512]{1,0:T(8,128)(2,1)} %bitcast.16, ...), custom_call_target="tpu_custom_call" | custom-call | tf_op jit(solution)/shard_map/pallas_call | solution.py:305
  57.1 0.0 copy-start.2
  57.1 1.9 %copy.17 = bf16[1,512,512]{2,1,0:T(8,128)(2,1)} copy(bf16[1,512,512]{2,1,0:T(8,128)(2,1)} %bitcast.13) | data formatting | bytes 1048576
  59.0 0.0 copy-done.2
  59.0 0.0 copy-start.1
  59.0 0.8 %copy.18 = bf16[1,512,512]{2,1,0:T(8,128)(2,1)} copy(bf16[1,512,512]{2,1,0:T(8,128)(2,1)S(1)} %bitcast.12) | data formatting | bytes 1048576
  59.8 0.4 copy-done.1
  60.2 0.0 copy-start
  60.2 0.8 %copy.19 = bf16[1,512,512]{2,1,0:T(8,128)(2,1)} copy(bf16[1,512,512]{2,1,0:T(8,128)(2,1)S(1)} %bitcast.11) | data formatting | bytes 1048576
  61.0 0.4 copy-done
  61.5 0.0 copy-start.3
  61.5 0.8 %copy.20 = bf16[1,512,512]{2,1,0:T(8,128)(2,1)} copy(bf16[1,512,512]{2,1,0:T(8,128)(2,1)S(1)} %bitcast.10) | data formatting | bytes 1048576
  62.2 0.2 copy-done.3
  62.5 0.7 %copy.21 = f32[32,1024]{1,0:T(8,128)} copy(f32[32,1024]{1,0:T(8,128)S(1)} %copy-done.3) | data formatting | bytes 262144
Async XLA Ops:
  57.1 1.9 %copy-start.2 = (bf16[512,512]{1,0:T(8,128)(2,1)S(1)}, bf16[512,512]{1,0:T(8,128)(2,1)}, u32[]{:S(2)}) copy-start(bf16[512,512]{1,0:T(8,128)(2,1)} %get-tuple-element.11) | copy-start | bytes 1572868
  59.0 1.2 %copy-start.1 = (bf16[512,512]{1,0:T(8,128)(2,1)S(1)}, bf16[512,512]{1,0:T(8,128)(2,1)}, u32[]{:S(2)}) copy-start(bf16[512,512]{1,0:T(8,128)(2,1)} %get-tuple-element.12) | copy-start | bytes 1572868
  60.2 1.2 %copy-start = (bf16[512,512]{1,0:T(8,128)(2,1)S(1)}, bf16[512,512]{1,0:T(8,128)(2,1)}, u32[]{:S(2)}) copy-start(bf16[512,512]{1,0:T(8,128)(2,1)} %get-tuple-element.13) | copy-start | bytes 1572868
  61.5 1.0 %copy-start.3 = (f32[32,1024]{1,0:T(8,128)S(1)}, f32[32,1024]{1,0:T(8,128)}, u32[]{:S(2)}) copy-start(f32[32,1024]{1,0:T(8,128)} %get-tuple-element.24) | copy-start | bytes 393220

commit v2 on v1

--- a/solution.py
+++ b/solution.py
@@ -20,17 +20,52 @@
     return lax.dot_general(a, b, (((ca,), (cb,)), ((), ())), preferred_element_type=F32)
 
 
+def routes(n, dp):
+    steps, dsteps = n.bit_length() - 1, dp.bit_length() - 1
+    plans = []
+    for at in (1, 2):
+        plan, split = [], False
+        for s in range(steps):
+            if s == at:
+                plan.append(("split", 0, n >> s, True))
+                split = True
+            plan.append(("hist", s, n >> (s + 1), split))
+        plan += [("both", s, 1, True) for s in range(1, dsteps)]
+        plan.append(("gather", 0, 1, True))
+        plans.append(plan)
+    return plans
+
+
 def kernel(
     n, dp, total_rows,
-    q_ref, k_ref, v_ref, u_ref, st_ref, w_ref, go_ref,
+    st_ref, q_hbm, k_hbm, v_hbm, u_hbm, w_hbm, go_hbm,
     dq_ref, dk_ref, dv_ref, du_ref, dw_ref,
+    q_ref, k_ref, v_ref, u_ref, w_ref, go_ref, in_sem,
     halo, w_s, g_s, att, dh, da, hid, out_kv, in_kv, wp, *rest,
 ):
     steps = n.bit_length() - 1
     dsteps = dp.bit_length() - 1
-    hops = steps + dsteps
-    sends, recvs = rest[:hops], rest[hops : 2 * hops]
-    ks, kr, gs, gr, ws, wr = rest[2 * hops :]
+    plans = routes(n, dp)
+    hops = len(plans[0])
+    count = 2 * hops
+    sends = (rest[:hops], rest[hops:count])
+    recvs = (rest[count : count + hops], rest[count + hops : 2 * count])
+    ks, kr, gs, gr, ws, wr = rest[2 * count :]
+    loads = [
+        pltpu.make_async_copy(src, dst, in_sem.at[i])
+        for i, (src, dst) in enumerate(
+            (
+                (k_hbm, k_ref),
+                (q_hbm, q_ref),
+                (v_hbm, v_ref),
+                (w_hbm, w_ref),
+                (go_hbm, go_ref),
+                (u_hbm, u_ref),
+            )
+        )
+    ]
+    for load in loads:
+        load.start()
     ev = q_ref.shape[0]
     blk = ev // 2
     me = lax.axis_index("hist")
@@ -42,8 +77,9 @@
     def xor(value, bit):
         return value + bit - 2 * bit * ((value // bit) % 2)
 
-    partners = [{"hist": xor(me, 1 << s)} for s in range(steps)]
-    partners += [{"dp": xor(mine, 1 << s)} for s in range(dsteps)]
+    hist_partners = [{"hist": xor(me, 1 << s)} for s in range(steps)]
+    dp_partners = [{"dp": xor(mine, 1 << s)} for s in range(dsteps)]
+    partners = hist_partners + dp_partners
 
     barrier = pltpu.get_barrier_semaphore()
     for partner in partners:
@@ -57,14 +93,14 @@
     def _():
         pl.semaphore_signal(barrier, inc=1, device_id={"hist": me - 1}, device_id_type=mesh)
 
-    pl.semaphore_wait(barrier, hops + has_left.astype(jnp.int32) + has_right.astype(jnp.int32))
+    pl.semaphore_wait(barrier, steps + dsteps + has_left.astype(jnp.int32) + has_right.astype(jnp.int32))
 
     halo_copies = [
         pltpu.make_async_remote_copy(
             src_ref=ref, dst_ref=halo.at[i], send_sem=ks.at[i], recv_sem=kr.at[i],
             device_id={"hist": me + 1}, device_id_type=mesh,
         )
-        for i, ref in enumerate((k_ref, v_ref))
+        for i, ref in enumerate((k_hbm, v_hbm))
     ]
     grad_copies = [
         pltpu.make_async_remote_copy(
@@ -74,11 +110,16 @@
         for h in range(HEADS)
     ]
     sum_copies = [
-        pltpu.make_async_remote_copy(
-            src_ref=sends[s], dst_ref=recvs[s], send_sem=ws.at[s], recv_sem=wr.at[s],
-            device_id=partners[s], device_id_type=mesh,
-        )
-        for s in range(hops)
+        [
+            pltpu.make_async_remote_copy(
+                src_ref=sends[c][i], dst_ref=recvs[c][i],
+                send_sem=ws.at[c * hops + i], recv_sem=wr.at[c * hops + i],
+                device_id=(hist_partners if kind == "hist" else dp_partners)[s],
+                device_id_type=mesh,
+            )
+            for i, (kind, s, _, _) in enumerate(plans[c])
+        ]
+        for c in range(2)
     ]
 
     @pl.when(has_right)
@@ -129,11 +170,15 @@
         cols = slice(b * blk, (b + 1) * blk)
         return dot(w_s[h, part, lo:hi, cols], values[lo:hi, head(h)], 0, 0)
 
+    for load in loads[:3]:
+        load.wait()
     for b in range(2):
         live = mask(1, b, *span(1, b))
         for h in range(HEADS):
             scores(1, b, h, k_ref, live)
             att[b * blk : (b + 1) * blk, head(h)] = mix(1, b, h, v_ref)
+    for load in loads[3:]:
+        load.wait()
     for b in range(2):
         rows = slice(b * blk, (b + 1) * blk)
         dh[rows, :] = dot(go_ref[rows, :], w_ref[...], 1, 1)
@@ -175,33 +220,50 @@
         )
         da[rows, :] = d_attn.astype(BF)
 
-    block_rows = wp.shape[1]
+    block_rows = wp.shape[2]
+    width = wp.shape[3]
+    low = mine % 2
 
     def weight_part():
-        cols = hid.shape[1] // 2
-        for b in range(2):
-            piece = dot(hid[:, b * cols : (b + 1) * cols], go_ref[...], 0, 0)
-            wp[b * n // 2 : (b + 1) * n // 2] = piece.reshape(n // 2, block_rows, piece.shape[1])
-
-    def launch(s):
-        if s < steps:
-            count = n >> (s + 1)
+        for g in range(4):
+            piece = dot(hid[...], go_ref[:, g * width : (g + 1) * width], 0, 0)
+            wp[g] = piece.reshape(n, block_rows, width)
+
+    def groups(c, split):
+        return [2 * c + low] if split else [2 * c, 2 * c + 1]
+
+    def launch(c, i):
+        kind, s, size, split = plans[c][i]
+        target = sends[c][i]
+        if kind == "hist":
             bit = (me // (1 << s)) % 2
-            for i in range(count):
-                sends[s][i] = wp[2 * i + 1 - bit].astype(BF)
+            for a, g in enumerate(groups(c, split)):
+                for j in range(size):
+                    target[a, j] = wp[g, 2 * j + 1 - bit].astype(BF)
+        elif kind == "split":
+            for j in range(size):
+                target[0, j] = wp[2 * c + 1 - low, j].astype(BF)
         else:
-            sends[s][0] = wp[0].astype(BF)
-        sum_copies[s].start()
-
-    def land(s):
-        sum_copies[s].wait_recv()
-        if s < steps:
-            count = n >> (s + 1)
+            target[0, 0] = wp[2 * c + low, 0].astype(BF)
+        sum_copies[c][i].start()
+
+    def land(c, i):
+        kind, s, size, split = plans[c][i]
+        source = recvs[c][i]
+        sum_copies[c][i].wait_recv()
+        if kind == "hist":
             bit = (me // (1 << s)) % 2
-            for i in range(count):
-                wp[i] = wp[2 * i + bit] + recvs[s][i].astype(F32)
+            for a, g in enumerate(groups(c, split)):
+                for j in range(size):
+                    wp[g, j] = wp[g, 2 * j + bit] + source[a, j].astype(F32)
+        elif kind == "split":
+            for j in range(size):
+                wp[2 * c + low, j] = wp[2 * c + low, j] + source[0, j].astype(F32)
+        elif kind == "both":
+            wp[2 * c + low, 0] = sends[c][i][0, 0].astype(F32) + source[0, 0].astype(F32)
         else:
-            wp[0] = sends[s][0].astype(F32) + recvs[s][0].astype(F32)
+            wp[2 * c + low, 0] = sends[c][i][0, 0].astype(F32)
+            wp[2 * c + 1 - low, 0] = source[0, 0].astype(F32)
 
     def queries(part, kb):
         return slice(0, (kb + 1) * blk) if part == 0 else slice(kb * blk, ev)
@@ -254,27 +316,44 @@
         dk_ref[:, head(h)] = (att[:, head(h)] + in_kv[h, 0].astype(F32)).astype(BF)
         dv_ref[:, head(h)] = (dh[:, head(h)] + in_kv[h, 1].astype(F32)).astype(BF)
 
+    pending = 0
+
+    def advance():
+        nonlocal pending
+        if pending < hops - 1:
+            for c in range(2):
+                land(c, pending)
+                launch(c, pending + 1)
+            pending += 1
+
     weight_part()
-    launch(0)
-    work = [(far, 0), (far, 1), (far, 2), (far, 3)]
-    work += [(near, 0), (near, 1), (near, 2), (near, 3)]
-    work += [(query_side, 0), (query_side, 1), (query_side, 2), (query_side, 3)]
-    pending = 0
-    for i, (task, h) in enumerate(work):
-        task(h)
-        if i % 3 == 2 or i == 1:
-            if pending < hops - 1:
-                land(pending)
-                pending += 1
-                launch(pending)
+    launch(0, 0)
+    launch(1, 0)
+    far(0)
+    advance()
+    far(1)
+    far(2)
+    far(3)
+    advance()
+    near(0)
+    near(1)
+    advance()
+    near(2)
+    near(3)
+    advance()
+    for h in range(HEADS):
+        query_side(h)
+        if h == 2:
+            advance()
     while pending < hops - 1:
-        land(pending)
-        pending += 1
-        launch(pending)
+        advance()
     for h in range(HEADS):
         finish(h)
-    land(hops - 1)
-    dw_ref[...] = wp[0] / math.sqrt(total_rows)
+    root = math.sqrt(total_rows)
+    for c in range(2):
+        land(c, hops - 1)
+        for g in (2 * c, 2 * c + 1):
+            dw_ref[:, g * width : (g + 1) * width] = wp[g, 0] / root
 
     @pl.when(has_right)
     def _():
@@ -286,28 +365,48 @@
         for copy in grad_copies:
             copy.wait_send()
 
-    for copy in sum_copies:
-        copy.wait_send()
+    for copies in sum_copies:
+        for copy in copies:
+            copy.wait_send()
+
+
+def emit(*refs):
+    sems = refs[10]
+    copies = [pltpu.make_async_copy(refs[i], refs[5 + i], sems.at[i]) for i in range(5)]
+    for copy in copies:
+        copy.start()
+    for copy in copies:
+        copy.wait()
 
 
 def shards(n, dp, queries, key_rows, value_rows, gate_rows, user_start, w_out, out_grad):
     ev, width = queries.shape[1:]
     model = w_out.shape[1]
     block_rows = width // n
-    steps = n.bit_length() - 1
-    dsteps = dp.bit_length() - 1
-    hops = steps + dsteps
-    sizes = [n >> (s + 1) for s in range(steps)] + [1] * dsteps
-    legs = [pltpu.VMEM((size, block_rows, model), BF) for size in sizes]
-    rows = jax.ShapeDtypeStruct((ev, width), BF)
+    plans = routes(n, dp)
+    hops = len(plans[0])
+    legs = [
+        pltpu.VMEM((1 if split else 2, size, block_rows, model // 4), BF)
+        for plan in plans
+        for _, _, size, split in plan
+    ]
+    rows = pltpu.VMEM((ev, width), BF)
+    outs = (rows, rows, rows, rows, pltpu.VMEM((block_rows, model), F32))
     vmem = pl.BlockSpec(memory_space=pltpu.VMEM)
     dma = pltpu.SemaphoreType.DMA
     results = pl.pallas_call(
         functools.partial(kernel, n, dp, dp * n * ev),
-        out_shape=(rows, rows, rows, rows, jax.ShapeDtypeStruct((block_rows, model), F32)),
-        in_specs=[vmem] * 7,
+        out_shape=outs,
+        in_specs=[vmem] + [pl.BlockSpec(memory_space=pl.ANY)] * 6,
         out_specs=(vmem,) * 5,
         scratch_shapes=[
+            pltpu.VMEM((ev, width), BF),
+            pltpu.VMEM((ev, width), BF),
+            pltpu.VMEM((ev, width), BF),
+            pltpu.VMEM((ev, width), BF),
+            pltpu.VMEM((width, model), BF),
+            pltpu.VMEM((ev, model), BF),
+            dma((6,)),
             pltpu.VMEM((2, ev, width), BF),
             pltpu.VMEM((HEADS, 2, ev, ev), BF),
             pltpu.VMEM((HEADS, 2, ev, ev), BF),
@@ -317,17 +416,24 @@
             pltpu.VMEM((ev, width), BF),
             pltpu.VMEM((HEADS, 2, ev, HS), BF),
             pltpu.VMEM((HEADS, 2, ev, HS), BF),
-            pltpu.VMEM((n, block_rows, model), F32),
+            pltpu.VMEM((4, n, block_rows, model // 4), F32),
         ]
         + legs
         + legs
-        + [dma((2,)), dma((2,)), dma((HEADS,)), dma((HEADS,)), dma((hops,)), dma((hops,))],
+        + [dma((2,)), dma((2,)), dma((HEADS,)), dma((HEADS,)), dma((2 * hops,)), dma((2 * hops,))],
         compiler_params=pltpu.CompilerParams(
             collective_id=0, has_side_effects=True, vmem_limit_bytes=60 * 1024 * 1024
         ),
     )(
-        queries[0], key_rows[0], value_rows[0], gate_rows[0], user_start, w_out, out_grad[0]
+        user_start, queries[0], key_rows[0], value_rows[0], gate_rows[0], w_out, out_grad[0]
     )
+    results = pl.pallas_call(
+        emit,
+        out_shape=tuple(jax.ShapeDtypeStruct(o.shape, o.dtype) for o in outs),
+        in_specs=[vmem] * 5,
+        out_specs=(pl.BlockSpec(memory_space=pl.ANY),) * 5,
+        scratch_shapes=[dma((5,))],
+    )(*[pltpu.with_memory_space_constraint(r, pltpu.VMEM) for r in results])
     return tuple(r[None] for r in results[:4]) + (results[4],)
 
 

time: 63.4 us -> 53.7 us (0.85)
  the two profiles are of different devices: /device:TPU:20 before, /device:TPU:0 now
where the time goes in v2:
time: 53.7 us; the launch traced here: 53.5 us
  Pallas kernels  52.9 us (99%)
  between operations  0.64 us (1%)
    pallas_call x1, Pallas kernels, shards(): pl.pallas_call(functools.partial(kernel, n, dp, dp * n * ev), out_shape=o...  51.5 us
    pallas_call x1, Pallas kernels, shards(): pl.pallas_call(emit, out_shape=tuple((jax.ShapeDtypeStruct(o.shape, o.dty...  1.39 us

profile of v2, /device:TPU:0, one launch (start us, length us, event | category | flops | bytes accessed | tf_op | source)
XLA Modules:
  0.0 53.5 jit_solution(12893382688958287164)
XLA Ops:
  0.6 51.5 %shard_map.110 = (bf16[512,512]{1,0:T(8,128)(2,1)S(1)}, bf16[512,512]{1,0:T(8,128)(2,1)S(1)}, bf16[512,512]{1,0:T(8,128)(2,1)S(1)}, bf16[512,512]{1,0:T(8,128)(2,1)S(1)}, f32[32,1024]{1,0:T(8,128)S(1)}) custom-call(s32[1,512]{1,0:T(1,128)} %st_ref.1, bf16[512,512]{1,0:T(8,128)(2,1)} %bitcast.10, bf16[512,512]{1,0:T(8,128)(2,1)} %bitcast.11, ...), custom_call_target="tpu_custom_call" | custom-call | tf_op jit(solution)/shard_map/pallas_call | solution.py:397
  52.1 1.4 %shard_map.111 = (bf16[512,512]{1,0:T(8,128)(2,1)}, bf16[512,512]{1,0:T(8,128)(2,1)}, bf16[512,512]{1,0:T(8,128)(2,1)}, bf16[512,512]{1,0:T(8,128)(2,1)}, f32[32,1024]{1,0:T(8,128)}) custom-call(bf16[512,512]{1,0:T(8,128)(2,1)S(1)} %get-tuple-element.15.refs_0_, bf16[512,512]{1,0:T(8,128)(2,1)S(1)} %get-tuple-element.16.refs_1_, ...), custom_call_target="tpu_custom_call" | custom-call | tf_op jit(solution)/shard_map/pallas_call | solution.py:430

commit v3 on v2

--- a/solution.py
+++ b/solution.py
@@ -200,7 +200,7 @@
         for h in range(HEADS):
             att[b * blk : (b + 1) * blk, head(h)] += mix(0, b, h, halo.at[1])
 
-    chunk = 64
+    chunk = 128
     @pl.loop(0, ev // chunk)
     def _(c):
         rows = pl.ds(pl.multiple_of(c * chunk, chunk), chunk)
@@ -225,9 +225,9 @@
     low = mine % 2
 
     def weight_part():
+        whole = dot(hid[...], go_ref[...], 0, 0)
         for g in range(4):
-            piece = dot(hid[...], go_ref[:, g * width : (g + 1) * width], 0, 0)
-            wp[g] = piece.reshape(n, block_rows, width)
+            wp[g] = whole[:, g * width : (g + 1) * width].reshape(n, block_rows, width)
 
     def groups(c, split):
         return [2 * c + low] if split else [2 * c, 2 * c + 1]
@@ -288,6 +288,7 @@
     def far(h):
         back(0, h, keep_far)
 
+    def give(h):
         @pl.when(has_left)
         def _():
             grad_copies[h].start()
@@ -330,21 +331,25 @@
     launch(0, 0)
     launch(1, 0)
     far(0)
+    far(1)
     advance()
-    far(1)
+    give(0)
     far(2)
     far(3)
+    near(0)
     advance()
-    near(0)
+    give(1)
     near(1)
-    advance()
     near(2)
     near(3)
     advance()
-    for h in range(HEADS):
-        query_side(h)
-        if h == 2:
-            advance()
+    give(2)
+    query_side(0)
+    query_side(1)
+    advance()
+    give(3)
+    query_side(2)
+    query_side(3)
     while pending < hops - 1:
         advance()
     for h in range(HEADS):

time: 53.7 us -> 47.4 us (0.88)
  the two profiles are of different devices: /device:TPU:0 before, /device:TPU:1 now
where the time goes in v3:
time: 47.4 us; the launch traced here: 47.3 us
  Pallas kernels  46.6 us (98%)
  between operations  0.64 us (1%)
    pallas_call x1, Pallas kernels, shards(): pl.pallas_call(functools.partial(kernel, n, dp, dp * n * ev), out_shape=o...  45.2 us
    pallas_call x1, Pallas kernels, shards(): pl.pallas_call(emit, out_shape=tuple((jax.ShapeDtypeStruct(o.shape, o.dty...  1.39 us

profile of v3, /device:TPU:1, one launch (start us, length us, event | category | flops | bytes accessed | tf_op | source)
XLA Modules:
  0.0 47.3 jit_solution(11592155206754627587)
XLA Ops:
  0.6 45.2 %shard_map.110 = (bf16[512,512]{1,0:T(8,128)(2,1)S(1)}, bf16[512,512]{1,0:T(8,128)(2,1)S(1)}, bf16[512,512]{1,0:T(8,128)(2,1)S(1)}, bf16[512,512]{1,0:T(8,128)(2,1)S(1)}, f32[32,1024]{1,0:T(8,128)S(1)}) custom-call(s32[1,512]{1,0:T(1,128)} %st_ref.1, bf16[512,512]{1,0:T(8,128)(2,1)} %bitcast.10, bf16[512,512]{1,0:T(8,128)(2,1)} %bitcast.11, ...), custom_call_target="tpu_custom_call" | custom-call | tf_op jit(solution)/shard_map/pallas_call | solution.py:402
  45.9 1.4 %shard_map.111 = (bf16[512,512]{1,0:T(8,128)(2,1)}, bf16[512,512]{1,0:T(8,128)(2,1)}, bf16[512,512]{1,0:T(8,128)(2,1)}, bf16[512,512]{1,0:T(8,128)(2,1)}, f32[32,1024]{1,0:T(8,128)}) custom-call(bf16[512,512]{1,0:T(8,128)(2,1)S(1)} %get-tuple-element.15.refs_0_, bf16[512,512]{1,0:T(8,128)(2,1)S(1)} %get-tuple-element.16.refs_1_, ...), custom_call_target="tpu_custom_call" | custom-call | tf_op jit(solution)/shard_map/pallas_call | solution.py:435

commit v4 on v3

--- a/solution.py
+++ b/solution.py
@@ -200,7 +200,7 @@
         for h in range(HEADS):
             att[b * blk : (b + 1) * blk, head(h)] += mix(0, b, h, halo.at[1])
 
-    chunk = 128
+    chunk = 256
     @pl.loop(0, ev // chunk)
     def _(c):
         rows = pl.ds(pl.multiple_of(c * chunk, chunk), chunk)
@@ -331,23 +331,23 @@
     launch(0, 0)
     launch(1, 0)
     far(0)
+    advance()
     far(1)
+    far(2)
+    far(3)
     advance()
     give(0)
-    far(2)
-    far(3)
     near(0)
+    near(1)
+    near(2)
     advance()
     give(1)
-    near(1)
-    near(2)
     near(3)
+    query_side(0)
     advance()
     give(2)
-    query_side(0)
+    give(3)
     query_side(1)
-    advance()
-    give(3)
     query_side(2)
     query_side(3)
     while pending < hops - 1:

time: 47.4 us -> 44.3 us (0.935)
  Pallas kernels: 46.6 us -> 43.5 us
    pallas_call x1, Pallas kernels: 45.2 us -> 42.1 us  [shards(): pl.pallas_call(functools.partial(kernel, n, dp, dp * n * ev), out_shape=o...]
where the time goes in v4:
time: 44.3 us; the launch traced here: 44.1 us
  Pallas kernels  43.5 us (98%)
  between operations  0.64 us (1%)
    pallas_call x1, Pallas kernels, shards(): pl.pallas_call(functools.partial(kernel, n, dp, dp * n * ev), out_shape=o...  42.1 us
    pallas_call x1, Pallas kernels, shards(): pl.pallas_call(emit, out_shape=tuple((jax.ShapeDtypeStruct(o.shape, o.dty...  1.39 us

profile of v4, /device:TPU:1, one launch (start us, length us, event | category | flops | bytes accessed | tf_op | source)
XLA Modules:
  0.0 44.1 jit_solution(14395740050155292587)
XLA Ops:
  0.6 42.1 %shard_map.110 = (bf16[512,512]{1,0:T(8,128)(2,1)S(1)}, bf16[512,512]{1,0:T(8,128)(2,1)S(1)}, bf16[512,512]{1,0:T(8,128)(2,1)S(1)}, bf16[512,512]{1,0:T(8,128)(2,1)S(1)}, f32[32,1024]{1,0:T(8,128)S(1)}) custom-call(s32[1,512]{1,0:T(1,128)} %st_ref.1, bf16[512,512]{1,0:T(8,128)(2,1)} %bitcast.10, bf16[512,512]{1,0:T(8,128)(2,1)} %bitcast.11, ...), custom_call_target="tpu_custom_call" | custom-call | tf_op jit(solution)/shard_map/pallas_call | solution.py:402
  42.7 1.4 %shard_map.111 = (bf16[512,512]{1,0:T(8,128)(2,1)}, bf16[512,512]{1,0:T(8,128)(2,1)}, bf16[512,512]{1,0:T(8,128)(2,1)}, bf16[512,512]{1,0:T(8,128)(2,1)}, f32[32,1024]{1,0:T(8,128)}) custom-call(bf16[512,512]{1,0:T(8,128)(2,1)S(1)} %get-tuple-element.15.refs_0_, bf16[512,512]{1,0:T(8,128)(2,1)S(1)} %get-tuple-element.16.refs_1_, ...), custom_call_target="tpu_custom_call" | custom-call | tf_op jit(solution)/shard_map/pallas_call | solution.py:435
